TPU v7x, 32 devices: a whole 2x2x4 slice. The times are simulated.
32 devices in a mesh: shot: 4 (over y, x), rcv: 8 (over z, core).
Axes of the slice: x: 2, y: 2, z: 4, core: 2. Of those that a mesh axis runs over, the one named last changes fastest.
Arguments:
- modeled: bfloat16 [2, 32, 4, 64, 512], P(None, 'shot', None, 'rcv'), may hold values from -9 to 9
- observed: bfloat16 [2, 4, 32, 64, 512], P(None, 'shot', 'rcv'), may hold values from -60 to 60
- mask: int32 [32, 4, 64], P('shot', None, 'rcv'), may hold values 0 or 1
- shot_order: int32 [32], replicated, may hold values from 0 to 31, as said below
- line_of_slot: int32 [4], replicated, may hold values from 0 to 3, as said below
- coupling: bfloat16 [2, 512, 512], replicated, may hold values from -0.25 to 0.25
- wavelet: float32 [2, 512], replicated, may hold values from -4 to 4
- damping: float32 [512], replicated, may hold values from 2048 to 32768
Outputs:
- new_wavelet: float32 [2, 512], replicated
- residual_out: bfloat16 [2, 32, 4, 64, 512], P(None, 'shot', None, 'rcv')
Inputs may be any that keep to these rules, and one draw needn't show every extreme that they name: Group g holds the shots shot_order[g * 8] to shot_order[(g + 1) * 8 - 1]; each shot number appears once. `line_of_slot`: each line appears in exactly one slot.
All inputs are finite; a program needn't handle non-finite values. No bound on the sum of `mask` on one device may be relied on, other than what follows from the above.
Results may differ from a plain program's by a relative error of at most 0.00045.
Values may be sent and summed in bfloat16 or wider, within the bound.
A program may use at most 64 MiB of HBM per device.

v0:
```python
import jax
import jax.numpy as jnp
from jax import lax
from jax.sharding import PartitionSpec as P


def weigh(trace, coupling):
    real_part = jnp.dot(trace[0], coupling[0], preferred_element_type=jnp.float32) - jnp.dot(
        trace[1], coupling[1], preferred_element_type=jnp.float32
    )
    imag_part = jnp.dot(trace[0], coupling[1], preferred_element_type=jnp.float32) + jnp.dot(
        trace[1], coupling[0], preferred_element_type=jnp.float32
    )
    return jnp.stack([real_part, imag_part])


def per_device(modeled, observed, mask, shot_order, line_of_slot, coupling, wavelet, damping):
    group_size = modeled.shape[1]
    line_count = modeled.shape[2]
    slot_count = lax.axis_size("shot")
    stored = observed[:, 0]
    spread = lax.all_to_all(stored, "rcv", split_axis=2, concat_axis=1, tiled=True)
    grouped = jnp.take(spread, shot_order, axis=1)
    grouped = grouped.reshape(2, slot_count, group_size, grouped.shape[2], grouped.shape[3])
    arrived = lax.all_to_all(grouped, "shot", split_axis=1, concat_axis=1, tiled=True)
    inverse = (
        jnp.zeros((line_count,), jnp.int32)
        .at[line_of_slot]
        .set(jnp.arange(line_count, dtype=jnp.int32))
    )
    by_line = jnp.transpose(jnp.take(arrived, inverse, axis=1), (0, 2, 1, 3, 4))
    wd = weigh(by_line, coupling)
    wg = weigh(modeled, coupling)
    live = mask.astype(jnp.float32)[..., None]
    res_re = live * (wd[0] - (wavelet[0] * wg[0] - wavelet[1] * wg[1]))
    res_im = live * (wd[1] - (wavelet[0] * wg[1] + wavelet[1] * wg[0]))
    num_re = jnp.sum(wg[0] * res_re + wg[1] * res_im, axis=(0, 1, 2))
    num_im = jnp.sum(wg[0] * res_im - wg[1] * res_re, axis=(0, 1, 2))
    den = jnp.sum(live * (wg[0] * wg[0] + wg[1] * wg[1]), axis=(0, 1, 2))
    numerator = jnp.stack([num_re, num_im])
    numerator, den = lax.psum((numerator, den), ("shot", "rcv"))
    new_wavelet = wavelet + numerator / (den + damping)[None, :]
    out_re = live * (wd[0] - (new_wavelet[0] * wg[0] - new_wavelet[1] * wg[1]))
    out_im = live * (wd[1] - (new_wavelet[0] * wg[1] + new_wavelet[1] * wg[0]))
    return (new_wavelet, jnp.stack([out_re, out_im]).astype(jnp.bfloat16))


def solution(mesh):
    placed = (
        P(None, "shot", None, "rcv", None),
        P(None, "shot", "rcv", None, None),
        P("shot", None, "rcv"),
        P(),
        P(),
        P(),
        P(),
        P(),
    )
    return jax.shard_map(
        per_device,
        mesh=mesh,
        in_specs=placed,
        out_specs=(P(), P(None, "shot", None, "rcv", None)),
        check_vma=False,
    )
```

profile of v0, /device:TPU:10, one launch (start us, length us, event | category | flops | bytes accessed | tf_op | source)
XLA Modules:
  0.0 82.5 jit_solution(1885239426793906169)
XLA Ops:
  0.6 0.0 copy-start
  0.6 2.3 %copy.30 = bf16[2,1,4,64,512]{4,2,0,3,1:T(4,128)(2,1)} copy(bf16[2,1,4,64,512]{4,3,2,1,0:T(8,128)(2,1)} %param.9) | data formatting | bytes 1048576 | tf_op args[1]
  3.0 5.5 %all-to-all-start = ((bf16[2,4,64,512]{3,1,0,2:T(4,128)(2,1)}), bf16[2,4,64,512]{3,1,0,2:T(4,128)(2,1)S(1)}, u32[]{:S(2)}, u32[]{:S(2)}) async-start(bf16[2,4,64,512]{3,1,0,2:T(4,128)(2,1)} %bitcast.71), calls=%async_computation | async-start | bytes 1048576 | tf_op jit(solution)/shard_map/all_to_all | solution.py:22
  8.4 0.0 copy-done.7
  8.4 0.0 copy-start.8
  8.5 0.6 copy-done.8
  9.1 0.1 broadcast_in_dim.31
  9.2 0.6 scatter_custom_fusion
  9.8 0.1 copy-done.3
  9.9 0.0 copy-done
  9.9 1.1 %fusion.2 = f32[8,4,8,512]{3,2,1,0:T(8,128)} fusion(bf16[2,512,512]{2,1,0:T(8,128)(2,1)S(1)} %copy-done, bf16[2,8,4,8,512]{4,3,2,1,0:T(8,128)(2,1)S(1)} %copy-done.1), kind=kOutput, calls=%fused_computation.10 | convolution fusion | flops 134217728 | bytes 1310720 | tf_op jit(solution)/shard_map/dot_general | solution.py:11
  11.0 0.3 fusion.10
  11.3 9.2 %all-to-all-done = bf16[2,4,64,512]{3,1,0,2:T(4,128)(2,1)S(1)} async-done(((bf16[2,4,64,512]{3,1,0,2:T(4,128)(2,1)}), bf16[2,4,64,512]{3,1,0,2:T(4,128)(2,1)S(1)}, u32[]{:S(2)}, u32[]{:S(2)}) %all-to-all-start) | async-done | bytes 524320 | tf_op jit(solution)/shard_map/all_to_all | solution.py:22
  20.5 0.2 copy.29
  20.7 0.6 gather_fusion
  21.3 0.9 %copy_select_fusion.1 = bf16[2,4,8,8,512]{4,3,2,0,1:T(8,128)(2,1)} fusion(bf16[2,4,8,8,512]{4,3,0,2,1:T(8,128)(2,1)S(1)} %bitcast.75, pred[4,8]{1,0:T(4,128)(4,1)S(1)} %broadcast_in_dim.31), kind=kLoop, calls=%fused_computation.22 | loop fusion | flops 262144 | bytes 1048608 | tf_op jit(solution)/shard_map/jit(_take)/select_n | solution.py:23
  22.3 4.4 %all-to-all-start.1 = ((bf16[2,4,8,8,512]{4,3,2,0,1:T(8,128)(2,1)}), bf16[2,4,8,8,512]{4,3,2,0,1:T(8,128)(2,1)S(1)}, u32[]{:S(2)}, u32[]{:S(2)}) async-start(bf16[2,4,8,8,512]{4,3,2,0,1:T(8,128)(2,1)} %copy_select_fusion.1), calls=%async_computation.1 | async-start | bytes 1048576 | tf_op jit(solution)/shard_map/all_to_all | solution.py:25
  26.7 0.3 convolution_subtract_fusion.1
  27.0 7.1 %all-to-all-done.1 = bf16[2,4,8,8,512]{4,3,2,0,1:T(8,128)(2,1)S(1)} async-done(((bf16[2,4,8,8,512]{4,3,2,0,1:T(8,128)(2,1)}), bf16[2,4,8,8,512]{4,3,2,0,1:T(8,128)(2,1)S(1)}, u32[]{:S(2)}, u32[]{:S(2)}) %all-to-all-start.1) | async-done | bytes 524320 | tf_op jit(solution)/shard_map/all_to_all | solution.py:25
  34.1 0.6 gather_fusion.1
  34.7 0.1 fusion.12
  34.8 0.3 fusion
  35.1 0.3 fusion.8
  35.4 0.3 convolution_add_fusion
  35.7 0.3 convolution_subtract_fusion
  36.0 0.7 copy-done.2
  36.8 1.4 %add_reduce_fusion = (f32[512]{0:T(512)S(1)}, f32[512]{0:T(512)S(1)}, f32[512]{0:T(512)S(1)}, f32[8,4,8,512]{3,2,1,0:T(8,128)}) fusion(f32[8,4,8,512]{3,2,1,0:T(8,128)S(1)} %convolution_add_fusion, f32[8,4,8,512]{3,2,1,0:T(8,128)S(1)} %convolution_subtract_fusion.1, f32[8,4,8,512]{3,2,1,0:T(8,128)S(1)} %convolution_subtract_fusion, f32[512]{0:T(512)S(1)} %bitcast.79, ...), kind=kOutput, calls=%fused_computation.29 | convolution fusion | flops 137361920 | bytes 3434496 | tf_op jit(solution)/shard_map/dot_general | solution.py:11
  38.2 41.5 %all-reduce = (f32[2,512]{1,0:T(2,128)S(1)}, f32[512]{0:T(512)S(1)}) all-reduce(f32[2,512]{1,0:T(2,128)S(1)} %pad_maximum_fusion.1, f32[512]{0:T(512)S(1)} %get-tuple-element.4), channel_id=1, replica_groups=mesh['shot'=4,'rcv'=8] {'shot','rcv'}, use_global_device_ids=true, to_apply=%region_3.4 | all-reduce | flops 1536 | bytes 12288 | tf_op jit(solution)/shard_map/psum | solution.py:41
  79.8 0.0 copy-start.4
  79.8 0.6 copy-done.4
  80.4 1.3 %fusion.21 = (bf16[1,8,4,8,512]{4,3,2,1,0:T(8,128)(2,1)S(1)}, bf16[1,8,4,8,512]{4,3,2,1,0:T(8,128)(2,1)S(1)}) fusion(f32[8,4,8,512]{3,2,1,0:T(8,128)S(1)} %convolution_subtract_fusion, f32[8,4,8,512]{3,2,1,0:T(8,128)} %get-tuple-element.13, f32[8,4,8,512]{3,2,1,0:T(8,128)S(1)} %convolution_subtract_fusion.1, f32[512]{0:T(512)S(1)} %bitcast.77, ...), kind=kLoop, calls=%fused_computation.40 | loop fusion | flops 1572864 | bytes 2626560 | tf_op jit(solution)/shard_map/stack | solution.py:45
  81.6 0.8 %pad_maximum_fusion = bf16[2,8,4,8,512]{4,3,2,1,0:T(8,128)(2,1)} fusion(bf16[1,8,4,8,512]{4,3,2,1,0:T(8,128)(2,1)S(1)} %get-tuple-element.8, bf16[1,8,4,8,512]{4,3,2,1,0:T(8,128)(2,1)S(1)} %get-tuple-element.7), kind=kLoop, calls=%fused_computation.7 | loop fusion | flops 262144 | bytes 1048576 | tf_op jit(solution)/shard_map/stack | solution.py:45
  (25 shorter events, 0.2 us)
Async XLA Ops:
  0.6 9.3 %copy-start = (bf16[2,512,512]{2,1,0:T(8,128)(2,1)S(1)}, bf16[2,512,512]{2,1,0:T(8,128)(2,1)}, u32[]{:S(2)}) copy-start(bf16[2,512,512]{2,1,0:T(8,128)(2,1)} %param.13) | copy-start | bytes 3145732
  3.0 5.5 %copy-start.7 = (s32[32]{0:T(128)S(1)}, s32[32]{0:T(128)}, u32[]{:S(2)}) copy-start(s32[32]{0:T(128)} %param.11) | copy-start | bytes 388
  3.0 6.9 %copy-start.1 = (bf16[2,8,4,8,512]{4,3,2,1,0:T(8,128)(2,1)S(1)}, bf16[2,8,4,8,512]{4,3,2,1,0:T(8,128)(2,1)}, u32[]{:S(2)}) copy-start(bf16[2,8,4,8,512]{4,3,2,1,0:T(8,128)(2,1)} %param.8) | copy-start | bytes 1572868
  3.0 17.6 %all-to-all-start = ((bf16[2,4,64,512]{3,1,0,2:T(4,128)(2,1)}), bf16[2,4,64,512]{3,1,0,2:T(4,128)(2,1)S(1)}, u32[]{:S(2)}, u32[]{:S(2)}) async-start(bf16[2,4,64,512]{3,1,0,2:T(4,128)(2,1)} %bitcast.71), calls=%async_computation | async-start | bytes 1048576 | tf_op jit(solution)/shard_map/all_to_all | solution.py:22
  8.4 0.7 copy-start.8
  9.2 0.7 copy-start.3
  22.2 4.4 %copy-start.5 = (s32[8,4,8]{2,1,0:T(4,128)S(1)}, s32[8,4,8]{2,1,0:T(4,128)}, u32[]{:S(2)}) copy-start(s32[8,4,8]{2,1,0:T(4,128)} %param.10) | copy-start | bytes 3076
  22.3 11.8 %all-to-all-start.1 = ((bf16[2,4,8,8,512]{4,3,2,0,1:T(8,128)(2,1)}), bf16[2,4,8,8,512]{4,3,2,0,1:T(8,128)(2,1)S(1)}, u32[]{:S(2)}, u32[]{:S(2)}) async-start(bf16[2,4,8,8,512]{4,3,2,0,1:T(8,128)(2,1)} %copy_select_fusion.1), calls=%async_computation.1 | async-start | bytes 1048576 | tf_op jit(solution)/shard_map/all_to_all | solution.py:25
  35.7 1.0 %copy-start.2 = (f32[8,4,8,512]{3,2,1,0:T(8,128)S(1)}, f32[8,4,8,512]{3,2,1,0:T(8,128)}, u32[]{:S(2)}) copy-start(f32[8,4,8,512]{3,2,1,0:T(8,128)} %fusion.2) | copy-start | bytes 1572868
  36.8 43.0 %copy-start.6 = (f32[512]{0:T(512)S(1)}, f32[512]{0:T(512)}, u32[]{:S(2)}) copy-start(f32[512]{0:T(512)} %param.15) | copy-start | bytes 6148
  79.8 0.6 copy-start.4
where the time goes:
time: 83 us; the launch traced here: 82.5 us
  blocking collectives  41.5 us (50%)
  waiting for transfers between devices  16.3 us (20%)
  starting transfers between devices  9.83 us (12%)
  local copies, waits for them, and re-layouts  6.43 us (8%)
  matrix products  4.33 us (5%)
  other arithmetic  3.19 us (4%)
    psum x1, blocking collectives, per_device(): numerator, den = lax.psum((numerator, den), ('shot', 'rcv'))  41.5 us
    all_to_all x1, waiting for transfers between devices, per_device(): lax.all_to_all(stored, 'rcv', split_axis=2, concat_axis=1, tiled=True)  9.24 us
    all_to_all x1, waiting for transfers between devices, per_device(): lax.all_to_all(grouped, 'shot', split_axis=1, concat_axis=1, tiled=True)  7.09 us
    all_to_all x1, starting transfers between devices, per_device(): lax.all_to_all(stored, 'rcv', split_axis=2, concat_axis=1, tiled=True)  5.45 us
    all_to_all x1, starting transfers between devices, per_device(): lax.all_to_all(grouped, 'shot', split_axis=1, concat_axis=1, tiled=True)  4.38 us
    unnamed x19, local copies, waits for them, and re-layouts  4.35 us
    another operation x2, other arithmetic, per_device(): return (new_wavelet, jnp.stack([out_re, out_im]).astype(jnp.bfloat16))  2.1 us
    dot_general x2, matrix products, weigh(): jnp.dot(trace[1], coupling[0], preferred_element_type=jnp.float32)  1.73 us
  transfers between devices with their start and end apart: 2, of which 2 were waited for; matrix products, arithmetic and copies ran while one was open for 3% of the time, Pallas kernels for 0%

commit v1 on v0

--- a/solution.py
+++ b/solution.py
@@ -38,7 +38,7 @@
     num_im = jnp.sum(wg[0] * res_im - wg[1] * res_re, axis=(0, 1, 2))
     den = jnp.sum(live * (wg[0] * wg[0] + wg[1] * wg[1]), axis=(0, 1, 2))
     numerator = jnp.stack([num_re, num_im])
-    numerator, den = lax.psum((numerator, den), ("shot", "rcv"))
+    numerator, den = lax.psum(lax.psum((numerator, den), "rcv"), "shot")
     new_wavelet = wavelet + numerator / (den + damping)[None, :]
     out_re = live * (wd[0] - (new_wavelet[0] * wg[0] - new_wavelet[1] * wg[1]))
     out_im = live * (wd[1] - (new_wavelet[0] * wg[1] + new_wavelet[1] * wg[0]))

time: 83 us -> 68.7 us (0.83)
  the two profiles are of different devices: /device:TPU:10 before, /device:TPU:0 now
where the time goes in v1:
time: 68.7 us; the launch traced here: 68.2 us
  blocking collectives  23.3 us (34%)
  waiting for transfers between devices  19.8 us (29%)
  starting transfers between devices  10.3 us (15%)
  local copies, waits for them, and re-layouts  6.43 us (9%)
  matrix products  4.32 us (6%)
  other arithmetic  3.19 us (5%)
  between operations  0.87 us (1%)
    psum x2, blocking collectives, per_device(): numerator, den = lax.psum(lax.psum((numerator, den), 'rcv'), 'shot')  23.3 us
    all_to_all x1, waiting for transfers between devices, per_device(): lax.all_to_all(stored, 'rcv', split_axis=2, concat_axis=1, tiled=True)  12.5 us
    all_to_all x1, waiting for transfers between devices, per_device(): lax.all_to_all(grouped, 'shot', split_axis=1, concat_axis=1, tiled=True)  7.38 us
    all_to_all x1, starting transfers between devices, per_device(): lax.all_to_all(stored, 'rcv', split_axis=2, concat_axis=1, tiled=True)  6.49 us
    unnamed x19, local copies, waits for them, and re-layouts  4.35 us
    all_to_all x1, starting transfers between devices, per_device(): lax.all_to_all(grouped, 'shot', split_axis=1, concat_axis=1, tiled=True)  3.85 us
    another operation x2, other arithmetic, per_device(): return (new_wavelet, jnp.stack([out_re, out_im]).astype(jnp.bfloat16))  2.1 us
    dot_general x2, matrix products, weigh(): jnp.dot(trace[1], coupling[0], preferred_element_type=jnp.float32)  1.73 us
  transfers between devices with their start and end apart: 2, of which 2 were waited for; matrix products, arithmetic and copies ran while one was open for 4% of the time, Pallas kernels for 0%

profile of v1, /device:TPU:0, one launch (start us, length us, event | category | flops | bytes accessed | tf_op | source)
XLA Modules:
  0.0 68.2 jit_solution(13861702024280165351)
XLA Ops:
  0.6 2.3 %copy.30 = bf16[2,1,4,64,512]{4,2,0,3,1:T(4,128)(2,1)} copy(bf16[2,1,4,64,512]{4,3,2,1,0:T(8,128)(2,1)} %param.9) | data formatting | bytes 1048576 | tf_op args[1]
  3.0 6.5 %all-to-all-start = ((bf16[2,4,64,512]{3,1,0,2:T(4,128)(2,1)}), bf16[2,4,64,512]{3,1,0,2:T(4,128)(2,1)S(1)}, u32[]{:S(2)}, u32[]{:S(2)}) async-start(bf16[2,4,64,512]{3,1,0,2:T(4,128)(2,1)} %bitcast.71), calls=%async_computation | async-start | bytes 1048576 | tf_op jit(solution)/shard_map/all_to_all | solution.py:22
  9.5 0.0 copy-start.8
  9.5 0.6 copy-done.8
  10.1 0.1 broadcast_in_dim.31
  10.2 0.6 scatter_custom_fusion
  10.9 0.1 copy-done.3
  10.9 0.0 copy-done
  10.9 1.1 %fusion.2 = f32[8,4,8,512]{3,2,1,0:T(8,128)} fusion(bf16[2,512,512]{2,1,0:T(8,128)(2,1)S(1)} %copy-done, bf16[2,8,4,8,512]{4,3,2,1,0:T(8,128)(2,1)S(1)} %copy-done.1), kind=kOutput, calls=%fused_computation.10 | convolution fusion | flops 134217728 | bytes 1310720 | tf_op jit(solution)/shard_map/dot_general | solution.py:11
  12.0 0.3 fusion.10
  12.3 12.5 %all-to-all-done = bf16[2,4,64,512]{3,1,0,2:T(4,128)(2,1)S(1)} async-done(((bf16[2,4,64,512]{3,1,0,2:T(4,128)(2,1)}), bf16[2,4,64,512]{3,1,0,2:T(4,128)(2,1)S(1)}, u32[]{:S(2)}, u32[]{:S(2)}) %all-to-all-start) | async-done | bytes 524320 | tf_op jit(solution)/shard_map/all_to_all | solution.py:22
  24.8 0.2 copy.29
  25.0 0.6 gather_fusion
  25.6 0.9 %copy_select_fusion.1 = bf16[2,4,8,8,512]{4,3,2,0,1:T(8,128)(2,1)} fusion(bf16[2,4,8,8,512]{4,3,0,2,1:T(8,128)(2,1)S(1)} %bitcast.75, pred[4,8]{1,0:T(4,128)(4,1)S(1)} %broadcast_in_dim.31), kind=kLoop, calls=%fused_computation.22 | loop fusion | flops 262144 | bytes 1048608 | tf_op jit(solution)/shard_map/jit(_take)/select_n | solution.py:23
  26.5 3.8 %all-to-all-start.1 = ((bf16[2,4,8,8,512]{4,3,2,0,1:T(8,128)(2,1)}), bf16[2,4,8,8,512]{4,3,2,0,1:T(8,128)(2,1)S(1)}, u32[]{:S(2)}, u32[]{:S(2)}) async-start(bf16[2,4,8,8,512]{4,3,2,0,1:T(8,128)(2,1)} %copy_select_fusion.1), calls=%async_computation.1 | async-start | bytes 1048576 | tf_op jit(solution)/shard_map/all_to_all | solution.py:25
  30.4 0.0 copy-done.5
  30.4 0.3 convolution_subtract_fusion.1
  30.7 7.4 %all-to-all-done.1 = bf16[2,4,8,8,512]{4,3,2,0,1:T(8,128)(2,1)S(1)} async-done(((bf16[2,4,8,8,512]{4,3,2,0,1:T(8,128)(2,1)}), bf16[2,4,8,8,512]{4,3,2,0,1:T(8,128)(2,1)S(1)}, u32[]{:S(2)}, u32[]{:S(2)}) %all-to-all-start.1) | async-done | bytes 524320 | tf_op jit(solution)/shard_map/all_to_all | solution.py:25
  38.1 0.6 gather_fusion.1
  38.7 0.1 fusion.12
  38.8 0.3 fusion
  39.1 0.3 fusion.8
  39.4 0.3 convolution_add_fusion
  39.8 0.3 convolution_subtract_fusion
  40.1 0.7 %copy-done.2 = f32[8,4,8,512]{3,2,1,0:T(8,128)S(1)} copy-done((f32[8,4,8,512]{3,2,1,0:T(8,128)S(1)}, f32[8,4,8,512]{3,2,1,0:T(8,128)}, u32[]{:S(2)}) %copy-start.2) | copy-done | bytes 524312
  40.8 1.4 %add_reduce_fusion = (f32[512]{0:T(512)S(1)}, f32[512]{0:T(512)S(1)}, f32[512]{0:T(512)S(1)}, f32[8,4,8,512]{3,2,1,0:T(8,128)}) fusion(f32[8,4,8,512]{3,2,1,0:T(8,128)S(1)} %convolution_add_fusion, f32[8,4,8,512]{3,2,1,0:T(8,128)S(1)} %convolution_subtract_fusion.1, f32[8,4,8,512]{3,2,1,0:T(8,128)S(1)} %convolution_subtract_fusion, f32[512]{0:T(512)S(1)} %bitcast.79, ...), kind=kOutput, calls=%fused_computation.29 | convolution fusion | flops 137361920 | bytes 3434496 | tf_op jit(solution)/shard_map/dot_general | solution.py:11
  42.2 14.2 %all-reduce = (f32[2,512]{1,0:T(2,128)S(1)}, f32[512]{0:T(512)S(1)}) all-reduce(f32[2,512]{1,0:T(2,128)S(1)} %pad_maximum_fusion.1, f32[512]{0:T(512)S(1)} %get-tuple-element.4), channel_id=1, replica_groups=mesh['shot'=4,'rcv'=8] {'rcv'}, use_global_device_ids=true, to_apply=%region_3.4 | all-reduce | flops 1536 | bytes 12288 | tf_op jit(solution)/shard_map/psum | solution.py:41
  56.5 9.0 %all-reduce.1 = (f32[2,512]{1,0:T(2,128)S(1)}, f32[512]{0:T(512)S(1)}) all-reduce(f32[2,512]{1,0:T(2,128)S(1)} %get-tuple-element.5, f32[512]{0:T(512)S(1)} %get-tuple-element.6), channel_id=1, replica_groups=mesh['shot'=4,'rcv'=8] {'shot'}, use_global_device_ids=true, to_apply=%region_4.5 | all-reduce | flops 1536 | bytes 12288 | tf_op jit(solution)/shard_map/psum | solution.py:41
  65.5 0.0 copy-start.4
  65.6 0.6 copy-done.4
  66.1 1.3 %fusion.21 = (bf16[1,8,4,8,512]{4,3,2,1,0:T(8,128)(2,1)S(1)}, bf16[1,8,4,8,512]{4,3,2,1,0:T(8,128)(2,1)S(1)}) fusion(f32[8,4,8,512]{3,2,1,0:T(8,128)S(1)} %convolution_subtract_fusion, f32[8,4,8,512]{3,2,1,0:T(8,128)} %get-tuple-element.15, f32[8,4,8,512]{3,2,1,0:T(8,128)S(1)} %convolution_subtract_fusion.1, f32[512]{0:T(512)S(1)} %bitcast.77, ...), kind=kLoop, calls=%fused_computation.40 | loop fusion | flops 1572864 | bytes 2626560 | tf_op jit(solution)/shard_map/stack | solution.py:45
  67.4 0.8 %pad_maximum_fusion = bf16[2,8,4,8,512]{4,3,2,1,0:T(8,128)(2,1)} fusion(bf16[1,8,4,8,512]{4,3,2,1,0:T(8,128)(2,1)S(1)} %get-tuple-element.10, bf16[1,8,4,8,512]{4,3,2,1,0:T(8,128)(2,1)S(1)} %get-tuple-element.9), kind=kLoop, calls=%fused_computation.7 | loop fusion | flops 262144 | bytes 1048576 | tf_op jit(solution)/shard_map/stack | solution.py:45
  (26 shorter events, 0.2 us)
Async XLA Ops:
  0.6 10.3 %copy-start = (bf16[2,512,512]{2,1,0:T(8,128)(2,1)S(1)}, bf16[2,512,512]{2,1,0:T(8,128)(2,1)}, u32[]{:S(2)}) copy-start(bf16[2,512,512]{2,1,0:T(8,128)(2,1)} %param.13) | copy-start | bytes 3145732
  3.0 6.5 %copy-start.7 = (s32[32]{0:T(128)S(1)}, s32[32]{0:T(128)}, u32[]{:S(2)}) copy-start(s32[32]{0:T(128)} %param.11) | copy-start | bytes 388
  3.0 8.0 %copy-start.1 = (bf16[2,8,4,8,512]{4,3,2,1,0:T(8,128)(2,1)S(1)}, bf16[2,8,4,8,512]{4,3,2,1,0:T(8,128)(2,1)}, u32[]{:S(2)}) copy-start(bf16[2,8,4,8,512]{4,3,2,1,0:T(8,128)(2,1)} %param.8) | copy-start | bytes 1572868
  3.0 21.8 %all-to-all-start = ((bf16[2,4,64,512]{3,1,0,2:T(4,128)(2,1)}), bf16[2,4,64,512]{3,1,0,2:T(4,128)(2,1)S(1)}, u32[]{:S(2)}, u32[]{:S(2)}) async-start(bf16[2,4,64,512]{3,1,0,2:T(4,128)(2,1)} %bitcast.71), calls=%async_computation | async-start | bytes 1048576 | tf_op jit(solution)/shard_map/all_to_all | solution.py:22
  9.5 0.7 copy-start.8
  10.2 0.7 %copy-start.3 = (f32[2,512]{1,0:T(2,128)S(1)}, f32[2,512]{1,0:T(2,128)}, u32[]{:S(2)}) copy-start(f32[2,512]{1,0:T(2,128)} %param.14) | copy-start | bytes 12292
  26.5 3.9 %copy-start.5 = (s32[8,4,8]{2,1,0:T(4,128)S(1)}, s32[8,4,8]{2,1,0:T(4,128)}, u32[]{:S(2)}) copy-start(s32[8,4,8]{2,1,0:T(4,128)} %param.10) | copy-start | bytes 3076
  26.5 11.6 %all-to-all-start.1 = ((bf16[2,4,8,8,512]{4,3,2,0,1:T(8,128)(2,1)}), bf16[2,4,8,8,512]{4,3,2,0,1:T(8,128)(2,1)S(1)}, u32[]{:S(2)}, u32[]{:S(2)}) async-start(bf16[2,4,8,8,512]{4,3,2,0,1:T(8,128)(2,1)} %copy_select_fusion.1), calls=%async_computation.1 | async-start | bytes 1048576 | tf_op jit(solution)/shard_map/all_to_all | solution.py:25
  39.7 1.0 %copy-start.2 = (f32[8,4,8,512]{3,2,1,0:T(8,128)S(1)}, f32[8,4,8,512]{3,2,1,0:T(8,128)}, u32[]{:S(2)}) copy-start(f32[8,4,8,512]{3,2,1,0:T(8,128)} %fusion.2) | copy-start | bytes 1572868
  40.8 24.7 %copy-start.6 = (f32[512]{0:T(512)S(1)}, f32[512]{0:T(512)}, u32[]{:S(2)}) copy-start(f32[512]{0:T(512)} %param.15) | copy-start | bytes 6148
  65.5 0.6 copy-start.4
